TPU v7x, 32 devices: a whole 2x2x4 slice. The times are simulated.
32 devices in a mesh: gx: 16 (over z, y, x), gy: 2 (over core).
Axes of the slice: x: 2, y: 2, z: 4, core: 2. Of those that a mesh axis runs over, the one named last changes fastest.
Arguments:
- coarse_state: float32 [24, 256, 256], P(None, 'gx', 'gy'), may hold values from -6 to 6
- coarse_rate: float32 [256, 256], P('gx', 'gy'), may hold values from 0.5 to 2
- fine_state: float32 [128, 24, 16, 256], P(('gx', 'gy')), may hold values from -6 to 6
- fine_rate: float32 [128, 16, 256], P(('gx', 'gy')), may hold values from 0.5 to 2
- refine_to: int32 [128], P(('gx', 'gy')), may hold values from -1 to 3, as said below
- parent_of: int32 [128], P(('gx', 'gy')), may hold values from -1 to 3, as said below
- kappa: float32 [24], replicated, may hold values from 0.01 to 0.05
- reaction: float32 [24, 24], replicated, may hold values from -1.25 to 1.25
Outputs:
- coarse_out: float32 [24, 256, 256], P(None, 'gx', 'gy')
- fine_out: float32 [128, 24, 16, 256], P(('gx', 'gy'))
Inputs may be any that keep to these rules, and one draw needn't show every extreme that they name: `refine_to`: -1 for a parent that is not refined; else k, the slot of its fine patch on the device k // 2 places higher along gx (wrapping), same gy index; no two parents name the same slot. `parent_of`: -1 for an empty slot; else p, its parent on the device k // 2 places lower along gx (wrapping), same gy index, k being the slot within its device; the two maps are inverse to each other; a device holds up to 4 live slots and in every draw some device holds that many.
All inputs are finite; a program needn't handle non-finite values.
Results may differ from a plain program's by a relative error of at most 0.0003.
Values sent between devices are 32-bit elements; how exact they have to be, the bound alone decides.
A program may use at most 64 MiB of HBM per device.

v0:
```python
import jax
import jax.numpy as jnp
from jax import lax
from jax.sharding import PartitionSpec as P

CY = 16
SUBSTEPS = 4


highest_mode = lax.Precision.HIGHEST


def padded_2(shard, sides, width):
    for axis, dim in sides:
        devices, length = (lax.axis_size(axis), shard.shape[dim])
        up = [(i, (i + 1) % devices) for i in range(devices)]
        down = [(j, i) for i, j in up]
        last = lax.slice_in_dim(shard, length - width, length, axis=dim)
        leading = lax.slice_in_dim(shard, 0, width, axis=dim)
        before = lax.ppermute(last, axis, up)
        after = lax.ppermute(leading, axis, down)
        shard = jnp.concatenate([before, shard, after], axis=dim)
    return shard


def shifted(value, axis, steps):
    count = lax.axis_size(axis)
    pairs = [(source, (source + steps) % count) for source in range(count)]
    return lax.ppermute(value, axis, pairs)


def roll_depth(center, depth, upward):
    position = jnp.arange(center.shape[-1], dtype=jnp.int32) % depth
    if upward:
        return jnp.where(
            position == depth - 1,
            jnp.roll(center, depth - 1, axis=-1),
            jnp.roll(center, -1, axis=-1),
        )
    return jnp.where(
        position == 0, jnp.roll(center, 1 - depth, axis=-1), jnp.roll(center, 1, axis=-1)
    )


def transport(padded, diffusion, courant, depth):
    center = padded[..., 1:-1, depth:-depth]
    lateral = (
        padded[..., 2:, depth:-depth]
        + padded[..., :-2, depth:-depth]
        + padded[..., 1:-1, 2 * depth :]
        + padded[..., 1:-1, : -2 * depth]
    )
    lower_z = roll_depth(center, depth, False)
    upper_z = roll_depth(center, depth, True)
    laplacian = lateral + lower_z + upper_z - 6.0 * center
    return center + diffusion * laplacian - courant * (center - lower_z)


def react(fields, rate_field, time_step, reaction):
    for substep in range(SUBSTEPS):
        fields = fields + time_step / SUBSTEPS * rate_field * jnp.einsum(
            "fg,...gxm->...fxm", reaction, fields, precision=highest_mode
        )
    return fields


def spread_table(coarse_cols, depth):
    source = jnp.arange(coarse_cols * depth, dtype=jnp.int32)
    target = jnp.arange(4 * coarse_cols * depth, dtype=jnp.int32)
    fine_depth = 2 * depth
    same = (target // fine_depth // 2 == source[:, None] // depth) & (
        target % fine_depth // 2 == source[:, None] % depth
    )
    return same.astype(jnp.float32)


def mean_table(fine_cols, depth):
    fine_depth = 2 * depth
    source = jnp.arange(fine_cols * fine_depth, dtype=jnp.int32)
    target = jnp.arange(fine_cols // 2 * depth, dtype=jnp.int32)
    same = (source[:, None] // fine_depth // 2 == target[None, :] // depth) & (
        source[:, None] % fine_depth // 2 == target[None, :] % depth
    )
    return 0.125 * same.astype(jnp.float32)


def pad_from_cycle(patches, cycle_now, depth):
    coarse_cols = cycle_now.shape[-1] // depth
    table = spread_table(coarse_cols, depth)
    widened = jnp.einsum("...m,mn->...n", cycle_now, table, precision=highest_mode)
    widened = jnp.repeat(widened, 2, axis=-2)
    fine_depth = 2 * depth
    cut = widened[..., 1:-1, fine_depth:-fine_depth]
    return cut.at[..., 1:-1, fine_depth:-fine_depth].set(patches)


def advance(patches, patch_rates, cycle_list, depth, kappa, reaction):
    for cycle_now in cycle_list:
        padded = pad_from_cycle(patches, cycle_now, depth)
        patches = react(
            transport(padded, 2.0 * kappa[:, None, None], 0.25, 2 * depth),
            patch_rates[:, None],
            0.5,
            reaction,
        )
    return patches


def coarse_means(patches, depth):
    count, fields, size_x, merged = patches.shape
    paired = patches.reshape(count, fields, size_x // 2, 2, merged).sum(axis=3)
    table = mean_table(merged // (2 * depth), depth)
    return jnp.einsum("...m,mn->...n", paired, table, precision=highest_mode)


def pad_coarse(field, depth):
    rows = padded_2(field, (("gx", 1),), 1)
    return padded_2(rows, (("gy", 2),), depth)


def expand_mask(mask, extra):
    return mask.reshape(mask.shape + (1,) * extra)


def body(coarse_state, coarse_rate, fine_state, fine_rate, refine_to, parent_of, kappa, reaction):
    fields_count, local_x, merged_y = coarse_state.shape
    local_y = CY
    depth = merged_y // local_y
    slot_count = fine_state.shape[0]
    diffusion = kappa[:, None, None]
    padded_old = pad_coarse(coarse_state, depth)
    coarse_new = react(transport(padded_old, diffusion, 0.25, depth), coarse_rate, 1.0, reaction)
    padded_new = pad_coarse(coarse_new, depth)
    half_x = local_x // 2
    half_y = local_y // 2
    parents_here = 4
    cycle_cols = (half_y + 2) * depth

    def cut_cycles(padded):
        return jnp.stack(
            [
                padded[
                    :,
                    half_x * (parent // 2) : half_x * (parent // 2) + half_x + 2,
                    half_y * (parent % 2) * depth : half_y * (parent % 2) * depth + cycle_cols,
                ]
                for parent in range(parents_here)
            ]
        )

    cycles_old = cut_cycles(padded_old)
    cycles_new = cut_cycles(padded_new)
    slot_ids = jnp.arange(slot_count, dtype=jnp.int32)
    matches = refine_to[None, :] == slot_ids[:, None]
    has_parent = jnp.any(matches, axis=1)
    source_parent = jnp.sum(
        matches.astype(jnp.int32) * jnp.arange(parents_here, dtype=jnp.int32)[None, :], axis=1
    )
    live_slot = parent_of >= 0
    refined = refine_to >= 0
    chosen = jnp.maximum(refine_to, 0)
    both_levels = jnp.stack((cycles_old, cycles_new), axis=1)
    outgoing = jnp.where(
        expand_mask(has_parent, 4), jnp.take(both_levels, source_parent, axis=0), 0.0
    )
    pieces = [outgoing[0:2]]
    offset = 1
    pieces.append(shifted(outgoing[2 * offset : 2 * offset + 2], "gx", offset))
    incoming = jnp.concatenate(pieces, axis=0)
    cycle_list = (incoming[:, 0], 0.5 * (incoming[:, 0] + incoming[:, 1]))
    advanced = advance(fine_state, fine_rate, cycle_list, depth, kappa, reaction)
    fine_out = jnp.where(expand_mask(live_slot, 3), advanced, 0.0)
    averages = coarse_means(fine_out, depth)
    returned = [averages[0:2]]
    offset = 1
    returned.append(shifted(averages[2 * offset : 2 * offset + 2], "gx", -offset))
    averaged = jnp.take(jnp.concatenate(returned, axis=0), chosen, axis=0)
    block_cols = half_y * depth
    row_blocks = []
    for upper in range(2):
        col_blocks = []
        for right in range(2):
            parent = 2 * upper + right
            own = coarse_new[
                :,
                upper * half_x : (upper + 1) * half_x,
                right * block_cols : (right + 1) * block_cols,
            ]
            col_blocks.append(jnp.where(refined[parent], averaged[parent], own))
        row_blocks.append(jnp.concatenate(col_blocks, axis=-1))
    coarse_out = jnp.concatenate(row_blocks, axis=-2)
    return (coarse_out, fine_out)


def solution(mesh):
    in_specs = (
        P(None, "gx", "gy"),
        P("gx", "gy"),
        P(("gx", "gy"), None, None, None),
        P(("gx", "gy"), None, None),
        P(("gx", "gy")),
        P(("gx", "gy")),
        P(),
        P(),
    )
    out_specs = (P(None, "gx", "gy"), P(("gx", "gy"), None, None, None))
    return jax.shard_map(body, mesh=mesh, in_specs=in_specs, out_specs=out_specs, check_vma=False)
```

profile of v0, /device:TPU:0, one launch (start us, length us, event | category | flops | bytes accessed | tf_op | source)
XLA Modules:
  0.0 148.7 jit_solution(807650519231152579)
XLA Ops:
  0.6 1.0 copy.106
  1.7 3.0 %collective-permute-start = (f32[24,1,128]{2,0,1:T(8,128)S(1)}, f32[24,1,128]{2,0,1:T(8,128)S(1)}, u32[]{:S(2)}, u32[]{:S(2)}) collective-permute-start(f32[24,1,128]{2,0,1:T(8,128)S(1)} %get-tuple-element.85), channel_id=1, source_target_pairs={{0,2},{2,4},{4,6},{6,8},{8,10},{10,12},{12,14},{14,16},{16,18},{18... | collective-permute-start | bytes 36872 | tf_op jit(solution)/shard_map/ppermute | solution.py:20
  4.7 4.1 %collective-permute-start.1 = (f32[24,1,128]{2,0,1:T(8,128)S(1)}, f32[24,1,128]{2,0,1:T(8,128)S(1)}, u32[]{:S(2)}, u32[]{:S(2)}) collective-permute-start(f32[24,1,128]{2,0,1:T(8,128)S(1)} %get-tuple-element.84), channel_id=1, source_target_pairs={{2,0},{4,2},{6,4},{8,6},{10,8},{12,10},{14,12},{16,14},{18,16},{20... | collective-permute-start | bytes 36872 | tf_op jit(solution)/shard_map/ppermute | solution.py:21
  12.2 2.2 %fusion.136 = (f32[4,24,16,241]{3,1,2,0:T(8,128)}, f32[4,24,16,241]{3,1,2,0:T(8,128)}) fusion(f32[4,24,16,256]{3,1,2,0:T(8,128)S(1)} %copy.133), kind=kLoop, calls=%fused_computation.250 | loop fusion | bytes 5922816 | tf_op jit(solution)/shard_map/jit(_roll_static)/slice | solution.py:41
  14.4 2.2 %fusion.139 = (f32[4,24,16,255]{3,1,2,0:T(8,128)}, f32[4,24,16,255]{3,1,2,0:T(8,128)}) fusion(f32[4,24,16,256]{3,1,2,0:T(8,128)S(1)} %copy.133), kind=kLoop, calls=%fused_computation.253 | loop fusion | bytes 6266880 | tf_op jit(solution)/shard_map/jit(_roll_static)/slice | solution.py:41
  16.6 1.5 %fusion.137 = (f32[4,24,16,15]{3,1,2,0:T(8,128)}, f32[4,24,16,15]{3,1,2,0:T(8,128)}) fusion(f32[4,24,16,256]{3,1,2,0:T(8,128)S(1)} %copy.133), kind=kLoop, calls=%fused_computation.251 | loop fusion | bytes 368640 | tf_op jit(solution)/shard_map/jit(_roll_static)/slice | solution.py:41
  27.4 5.6 %collective-permute-start.5 = (f32[24,1,128]{2,0,1:T(8,128)S(1)}, f32[24,1,128]{2,0,1:T(8,128)S(1)}, u32[]{:S(2)}, u32[]{:S(2)}) collective-permute-start(f32[24,1,128]{2,0,1:T(8,128)S(1)} %get-tuple-element.75), channel_id=1, source_target_pairs={{2,0},{4,2},{6,4},{8,6},{10,8},{12,10},{14,12},{16,14},{18,16},{20... | collective-permute-start | bytes 36872 | tf_op jit(solution)/shard_map/ppermute | solution.py:21
  33.3 1.4 collective-permute-done.4
  38.8 1.4 fusion.138
  40.2 15.8 %collective-permute-done.8 = f32[2,2,24,10,80]{4,2,3,1,0:T(8,128)S(1)} collective-permute-done((f32[2,2,24,10,80]{4,2,3,1,0:T(8,128)S(1)}, f32[2,2,24,10,80]{4,2,3,1,0:T(8,128)S(1)}, u32[]{:S(2)}, u32[]{:S(2)}) %collective-permute-start.8) | collective-permute-done | bytes 307232 | tf_op jit(solution)/shard_map/ppermute | solution.py:29
  57.8 2.2 %slice.439 = f32[4,24,18,288]{3,1,2,0:T(8,128)} slice(f32[4,24,20,320]{3,1,2,0:T(8,128)S(1)} %bitcast.160), slice={[0:4], [0:24], [1:19], [16:304]} | slice | bytes 3981312 | tf_op jit(solution)/shard_map/slice | solution.py:93
  60.0 18.4 %scatter.6 = f32[4,24,18,288]{3,1,2,0:T(8,128)} dynamic-update-slice(f32[4,24,18,288]{3,1,2,0:T(8,128)} %slice.439, f32[4,24,16,256]{3,1,2,0:T(8,128)S(1)} %copy.133, s32[]{:T(128)} %constant.261.clone.1, s32[]{:T(128)} %constant.261.clone.1, s32[]{:T(128)} %constant.272.clone.1, s32[]{:T(128)} %constant.275.clone.1) | dynamic-update-slice | bytes 3145732 | tf_op jit(solution)/shard_map/scatter | solution.py:94
  78.5 8.5 %fusion.11 = f32[4,24,16,256]{3,1,2,0:T(8,128)S(1)} fusion(f32[4,24,18,288]{3,1,2,0:T(8,128)} %scatter.6, f32[4,24,16,241]{3,1,2,0:T(8,128)} %get-tuple-element.43, f32[4,24,16,15]{3,1,2,0:T(8,128)} %get-tuple-element.45, f32[4,24,16,1]{3,1,2,0:T(8,128)} %get-tuple-element.47, f32[4,24,16,255]{3,1,2,0:T(8,128)} %get-tuple-element.49, ...), kind=kLoop, calls=%fused_computation.17 | loop fusion | flops 7077888 | bytes 15729248 | tf_op jit(solution)/shard_map/sub | solution.py:56
  86.9 1.5 fusion.101
  88.4 1.9 %bitcast_add_fusion.6 = f32[4,24,16,256]{3,1,2,0:T(8,128)S(1)} fusion(f32[4,24,16,256]{3,1,2,0:T(8,128)S(1)} %fusion.11, f32[4,16,256,24]{2,3,1,0:T(8,128)S(1)} %fusion.101, f32[4,16,256]{2,1,0:T(8,128)S(1)} %copy-done.9, f32[24,24]{1,0:T(8,128)S(1)} %copy-done), kind=kOutput, calls=%fused_computation.31 | convolution fusion | flops 115605504 | bytes 4786432 | tf_op jit(solution)/shard_map/fg,...gxm->...fxm/dot_general | solution.py:61
  90.3 1.5 fusion.98
  91.8 1.9 %bitcast_add_fusion.4 = f32[4,24,16,256]{3,1,2,0:T(8,128)S(1)} fusion(f32[4,24,16,256]{3,1,2,0:T(8,128)S(1)} %bitcast_add_fusion.6, f32[4,16,256,24]{2,3,1,0:T(8,128)S(1)} %fusion.98, f32[4,16,256]{2,1,0:T(8,128)S(1)} %copy-done.9, f32[24,24]{1,0:T(8,128)S(1)} %copy-done), kind=kOutput, calls=%fused_computation.29 | convolution fusion | flops 115605504 | bytes 4786432 | tf_op jit(solution)/shard_map/fg,...gxm->...fxm/dot_general | solution.py:61
  93.6 1.7 %fusion.132 = (f32[4,24,16,241]{3,1,2,0:T(8,128)S(1)}, f32[4,24,16,241]{3,1,2,0:T(8,128)}) fusion(f32[4,24,16,256]{3,1,2,0:T(8,128)S(1)} %bitcast_add_fusion.4), kind=kLoop, calls=%fused_computation.246 | loop fusion | bytes 5922816 | tf_op jit(solution)/shard_map/jit(_roll_static)/slice | solution.py:41
  95.3 2.2 %fusion.135 = (f32[4,24,16,255]{3,1,2,0:T(8,128)}, f32[4,24,16,255]{3,1,2,0:T(8,128)}) fusion(f32[4,24,16,256]{3,1,2,0:T(8,128)S(1)} %bitcast_add_fusion.4), kind=kLoop, calls=%fused_computation.249 | loop fusion | bytes 6266880 | tf_op jit(solution)/shard_map/jit(_roll_static)/slice | solution.py:41
  97.5 1.4 fusion.133
  98.9 1.5 %fusion.134 = (f32[4,24,16,1]{3,1,2,0:T(8,128)}, f32[4,24,16,1]{3,1,2,0:T(8,128)}) fusion(f32[4,24,16,256]{3,1,2,0:T(8,128)S(1)} %bitcast_add_fusion.4), kind=kLoop, calls=%fused_computation.248 | loop fusion | bytes 24576 | tf_op jit(solution)/shard_map/jit(_roll_static)/slice | solution.py:41
  101.4 2.2 %slice.452 = f32[4,24,18,288]{3,1,2,0:T(8,128)} slice(f32[4,24,20,320]{3,1,2,0:T(8,128)S(1)} %bitcast.161), slice={[0:4], [0:24], [1:19], [16:304]} | slice | bytes 3981312 | tf_op jit(solution)/shard_map/slice | solution.py:93
  103.6 18.1 %scatter.9 = f32[4,24,18,288]{3,1,2,0:T(8,128)} dynamic-update-slice(f32[4,24,18,288]{3,1,2,0:T(8,128)} %slice.452, f32[4,24,16,256]{3,1,2,0:T(8,128)S(1)} %bitcast_add_fusion.4, s32[]{:T(128)} %constant.261.clone.1, s32[]{:T(128)} %constant.261.clone.1, s32[]{:T(128)} %constant.272.clone.1, s32[]{:T(128)} %constant.275.clone.1) | dynamic-update-slice | bytes 3145732 | tf_op jit(solution)/shard_map/scatter | solution.py:94
  121.8 7.9 %fusion.5 = f32[4,24,16,256]{3,1,2,0:T(8,128)S(1)} fusion(f32[4,24,16,256]{3,1,2,0:T(8,128)S(1)} %bitcast_add_fusion.4, f32[4,24,18,288]{3,1,2,0:T(8,128)} %scatter.9, f32[4,24,16,241]{3,1,2,0:T(8,128)} %get-tuple-element.35, f32[4,24,16,15]{3,1,2,0:T(8,128)} %get-tuple-element.37, f32[4,24,16,1]{3,1,2,0:T(8,128)} %get-tuple-element.39, ...), kind=kLoop, calls=%fused_computation.8 | loop fusion | flops 7077888 | bytes 15729248 | tf_op jit(solution)/shard_map/sub | solution.py:56
  129.7 1.5 fusion.95
  131.1 1.9 %bitcast_add_fusion.2 = f32[4,24,16,256]{3,1,2,0:T(8,128)S(1)} fusion(f32[4,24,16,256]{3,1,2,0:T(8,128)S(1)} %fusion.5, f32[4,16,256,24]{2,3,1,0:T(8,128)S(1)} %fusion.95, f32[4,16,256]{2,1,0:T(8,128)S(1)} %copy-done.9, f32[24,24]{1,0:T(8,128)S(1)} %copy-done), kind=kOutput, calls=%fused_computation.27 | convolution fusion | flops 115605504 | bytes 4786432 | tf_op jit(solution)/shard_map/fg,...gxm->...fxm/dot_general | solution.py:61
  133.0 1.5 fusion.92
  134.5 1.9 %fusion.12 = f32[4,24,16,256]{3,1,2,0:T(8,128)S(1)} fusion(f32[4,24,16,256]{3,1,2,0:T(8,128)S(1)} %bitcast_add_fusion.2, f32[4,16,256,24]{2,3,1,0:T(8,128)S(1)} %fusion.92, f32[4,16,256]{2,1,0:T(8,128)S(1)} %copy-done.9, pred[4]{0:T(512)(128)(4,1)S(1)} %copy-done.22, f32[24,24]{1,0:T(8,128)S(1)} %copy-done), kind=kOutput, calls=%fused_computation.25 | convolution fusion | flops 115998720 | bytes 4786436 | tf_op jit(solution)/shard_map/fg,...gxm->...fxm/dot_general | solution.py:61
  138.0 1.8 %collective-permute-start.9 = (f32[2,24,8,64]{3,2,1,0:T(8,128)S(1)}, f32[2,24,8,64]{3,2,1,0:T(8,128)S(1)}, u32[]{:S(2)}, u32[]{:S(2)}) collective-permute-start(f32[2,24,8,64]{3,2,1,0:T(8,128)S(1)} %get-tuple-element.65), channel_id=1, source_target_pairs={{0,30},{2,0},{4,2},{6,4},{8,6},{10,8},{12,10},{14,12},{16,14},{18,... | collective-permute-start | bytes 294920 | tf_op jit(solution)/shard_map/ppermute | solution.py:29
  139.8 1.6 %copy.138 = f32[4,24,16,256]{3,2,1,0:T(8,128)} copy(f32[4,24,16,256]{3,1,2,0:T(8,128)S(1)} %fusion.12) | data formatting | bytes 3145728
  141.4 3.0 %collective-permute-done.9 = f32[2,24,8,64]{3,2,1,0:T(8,128)S(1)} collective-permute-done((f32[2,24,8,64]{3,2,1,0:T(8,128)S(1)}, f32[2,24,8,64]{3,2,1,0:T(8,128)S(1)}, u32[]{:S(2)}, u32[]{:S(2)}) %collective-permute-start.9) | collective-permute-done | bytes 98336 | tf_op jit(solution)/shard_map/ppermute | solution.py:29
  145.2 2.7 %slice_select_fusion.3 = (f32[24,8,64]{2,0,1:T(8,128)S(1)}, f32[24,8,64]{2,0,1:T(8,128)S(1)}, f32[24,8,64]{2,0,1:T(8,128)S(1)}, f32[24,8,64]{2,0,1:T(8,128)S(1)}) fusion(f32[24,16,128]{2,0,1:T(8,128)S(1)} %copy-done.4, f32[4,24,8,64]{3,1,2,0:T(8,128)S(1)} %copy_select_fusion, pred[]{:T(512)} %bitcast, pred[]{:T(512)} %bitcast.44, pred[]{:T(512)} %bitcast.42, ...), kind=kLoop, calls=%fused_computation.121 | loop fusion | flops 49152 | bytes 589828 | tf_op jit(solution)/shard_map/jit(_where)/select_n | solution.py:189
  (123 shorter events, 22.8 us)
Async XLA Ops:
  0.6 24.8 %copy-start = (f32[24,24]{1,0:T(8,128)S(1)}, f32[24,24]{1,0:T(8,128)}, u32[]{:S(2)}) copy-start(f32[24,24]{1,0:T(8,128)} %param.19) | copy-start | bytes 6916
  1.7 21.7 %collective-permute-start = (f32[24,1,128]{2,0,1:T(8,128)S(1)}, f32[24,1,128]{2,0,1:T(8,128)S(1)}, u32[]{:S(2)}, u32[]{:S(2)}) collective-permute-start(f32[24,1,128]{2,0,1:T(8,128)S(1)} %get-tuple-element.85), channel_id=1, source_target_pairs={{0,2},{2,4},{4,6},{6,8},{8,10},{10,12},{12,14},{14,16},{16,18},{18... | collective-permute-start | bytes 36872 | tf_op jit(solution)/shard_map/ppermute | solution.py:20
  4.7 4.6 %copy-start.25 = (s32[4]{0:T(128)S(1)}, s32[4]{0:T(128)}, u32[]{:S(2)}) copy-start(s32[4]{0:T(128)} %param.16) | copy-start | bytes 52
  4.7 6.6 %copy-start.1 = (f32[4,24,16,256]{3,2,1,0:T(8,128)S(1)}, f32[4,24,16,256]{3,2,1,0:T(8,128)}, u32[]{:S(2)}) copy-start(f32[4,24,16,256]{3,2,1,0:T(8,128)} %param.14) | copy-start | bytes 4718596
  4.7 18.8 %collective-permute-start.1 = (f32[24,1,128]{2,0,1:T(8,128)S(1)}, f32[24,1,128]{2,0,1:T(8,128)S(1)}, u32[]{:S(2)}, u32[]{:S(2)}) collective-permute-start(f32[24,1,128]{2,0,1:T(8,128)S(1)} %get-tuple-element.84), channel_id=1, source_target_pairs={{2,0},{4,2},{6,4},{8,6},{10,8},{12,10},{14,12},{16,14},{18,16},{20... | collective-permute-start | bytes 36872 | tf_op jit(solution)/shard_map/ppermute | solution.py:21
  16.6 3.2 %copy-start.13 = (f32[16,128]{1,0:T(8,128)S(1)}, f32[16,128]{1,0:T(8,128)}, u32[]{:S(2)}) copy-start(f32[16,128]{1,0:T(8,128)} %param.13) | copy-start | bytes 24580
  16.6 3.8 %copy-start.21 = (f32[24]{0:T(128)S(1)}, f32[24]{0:T(128)}, u32[]{:S(2)}) copy-start(f32[24]{0:T(128)} %param.18) | copy-start | bytes 292
  16.6 4.4 %copy-start.11 = (f32[4,16,256]{2,1,0:T(8,128)S(1)}, f32[4,16,256]{2,1,0:T(8,128)}, u32[]{:S(2)}) copy-start(f32[4,16,256]{2,1,0:T(8,128)} %param.15) | copy-start | bytes 196612
  16.6 5.0 %copy-start.26 = (s32[4]{0:T(128)S(1)}, s32[4]{0:T(128)}, u32[]{:S(2)}) copy-start(s32[4]{0:T(128)} %param.17) | copy-start | bytes 52
  16.6 6.8 %copy-start.10 = (f32[24,16,128]{2,1,0:T(8,128)S(1)}, f32[24,16,128]{2,1,0:T(8,128)}, u32[]{:S(2)}) copy-start(f32[24,16,128]{2,1,0:T(8,128)} %param.12) | copy-start | bytes 589828
  23.6 1.5 %collective-permute-start.2 = (f32[24,18,8]{2,0,1:T(8,128)S(1)}, f32[24,18,8]{2,0,1:T(8,128)S(1)}, u32[]{:S(2)}, u32[]{:S(2)}) collective-permute-start(f32[24,18,8]{2,0,1:T(8,128)S(1)} %get-tuple-element.73), channel_id=1, source_target_pairs={{0,1},{1,0},{2,3},{3,2},{4,5},{5,4},{6,7},{7,6},{8,9},{9,8},{10,11... | collective-permute-start | bytes 41480 | tf_op jit(solution)/shard_map/ppermute | solution.py:20
  23.7 1.8 %collective-permute-start.3 = (f32[24,18,8]{2,0,1:T(8,128)S(1)}, f32[24,18,8]{2,0,1:T(8,128)S(1)}, u32[]{:S(2)}, u32[]{:S(2)}) collective-permute-start(f32[24,18,8]{2,0,1:T(8,128)S(1)} %get-tuple-element.72), channel_id=1, source_target_pairs={{1,0},{0,1},{3,2},{2,3},{5,4},{4,5},{7,6},{6,7},{9,8},{8,9},{11,10... | collective-permute-start | bytes 41480 | tf_op jit(solution)/shard_map/ppermute | solution.py:21
  27.3 9.4 %copy-start.3 = (f32[24,16,128]{2,0,1:T(8,128)}, f32[24,16,128]{2,0,1:T(8,128)S(1)}, u32[]{:S(2)}) copy-start(f32[24,16,128]{2,0,1:T(8,128)S(1)} %fusion.14) | copy-start | bytes 589828
  27.3 7.3 %collective-permute-start.4 = (f32[24,1,128]{2,0,1:T(8,128)S(1)}, f32[24,1,128]{2,0,1:T(8,128)S(1)}, u32[]{:S(2)}, u32[]{:S(2)}) collective-permute-start(f32[24,1,128]{2,0,1:T(8,128)S(1)} %get-tuple-element.74), channel_id=1, source_target_pairs={{0,2},{2,4},{4,6},{6,8},{8,10},{10,12},{12,14},{14,16},{16,18},{18... | collective-permute-start | bytes 36872 | tf_op jit(solution)/shard_map/ppermute | solution.py:20
  27.4 7.3 %collective-permute-start.5 = (f32[24,1,128]{2,0,1:T(8,128)S(1)}, f32[24,1,128]{2,0,1:T(8,128)S(1)}, u32[]{:S(2)}, u32[]{:S(2)}) collective-permute-start(f32[24,1,128]{2,0,1:T(8,128)S(1)} %get-tuple-element.75), channel_id=1, source_target_pairs={{2,0},{4,2},{6,4},{8,6},{10,8},{12,10},{14,12},{16,14},{18,16},{20... | collective-permute-start | bytes 36872 | tf_op jit(solution)/shard_map/ppermute | solution.py:21
  34.8 1.5 %collective-permute-start.6 = (f32[24,18,8]{2,0,1:T(8,128)S(1)}, f32[24,18,8]{2,0,1:T(8,128)S(1)}, u32[]{:S(2)}, u32[]{:S(2)}) collective-permute-start(f32[24,18,8]{2,0,1:T(8,128)S(1)} %get-tuple-element.70), channel_id=1, source_target_pairs={{0,1},{1,0},{2,3},{3,2},{4,5},{5,4},{6,7},{7,6},{8,9},{9,8},{10,11... | collective-permute-start | bytes 41480 | tf_op jit(solution)/shard_map/ppermute | solution.py:20
  34.9 1.8 %collective-permute-start.7 = (f32[24,18,8]{2,0,1:T(8,128)S(1)}, f32[24,18,8]{2,0,1:T(8,128)S(1)}, u32[]{:S(2)}, u32[]{:S(2)}) collective-permute-start(f32[24,18,8]{2,0,1:T(8,128)S(1)} %get-tuple-element.71), channel_id=1, source_target_pairs={{1,0},{0,1},{3,2},{2,3},{5,4},{4,5},{7,6},{6,7},{9,8},{8,9},{11,10... | collective-permute-start | bytes 41480 | tf_op jit(solution)/shard_map/ppermute | solution.py:21
  38.7 17.3 %copy-start.5 = (f32[2,2,24,10,80]{4,2,3,1,0:T(8,128)}, f32[2,2,24,10,80]{4,2,3,1,0:T(8,128)S(1)}, u32[]{:S(2)}) copy-start(f32[2,2,24,10,80]{4,2,3,1,0:T(8,128)S(1)} %get-tuple-element.51) | copy-start | bytes 921604
  38.7 17.3 %collective-permute-start.8 = (f32[2,2,24,10,80]{4,2,3,1,0:T(8,128)S(1)}, f32[2,2,24,10,80]{4,2,3,1,0:T(8,128)S(1)}, u32[]{:S(2)}, u32[]{:S(2)}) collective-permute-start(f32[2,2,24,10,80]{4,2,3,1,0:T(8,128)S(1)} %get-tuple-element.50), channel_id=1, source_target_pairs={{0,2},{2,4},{4,6},{6,8},{8,10},{10,12},{12,14},{14,16},{16,18},{18... | collective-permute-start | bytes 921608 | tf_op jit(solution)/shard_map/ppermute | solution.py:29
  38.8 17.9 %copy-start.12 = (s32[320]{0:T(512)S(1)}, s32[320]{0:T(512)}, u32[]{:S(2)}) copy-start(s32[320]{0:T(512)} %get-tuple-element.95) | copy-start | bytes 3844
  38.8 17.9 %copy-start.17 = (s32[80]{0:T(128)S(1)}, s32[80]{0:T(128)}, u32[]{:S(2)}) copy-start(s32[80]{0:T(128)} %get-tuple-element.96) | copy-start | bytes 964
  38.8 17.9 %copy-start.18 = (s32[80]{0:T(128)S(1)}, s32[80]{0:T(128)}, u32[]{:S(2)}) copy-start(s32[80]{0:T(128)} %get-tuple-element.97) | copy-start | bytes 964
  60.0 18.4 %copy-start.2 = (f32[4,24,16,256]{3,2,1,0:T(8,128)S(1)}, f32[4,24,16,256]{3,2,1,0:T(8,128)}, u32[]{:S(2)}) copy-start(f32[4,24,16,256]{3,2,1,0:T(8,128)} %param.14) | copy-start | bytes 4718596
  60.0 18.4 %copy-start.16 = (f32[24]{0:T(128)S(1)}, f32[24]{0:T(128)}, u32[]{:S(2)}) copy-start(f32[24]{0:T(128)} %broadcast_multiply_fusion.2) | copy-start | bytes 292
  60.0 18.4 %copy-start.19 = (pred[256]{0:T(512)(128)(4,1)S(1)}, pred[256]{0:T(512)(128)(4,1)}, u32[]{:S(2)}) copy-start(pred[256]{0:T(512)(128)(4,1)} %get-tuple-element.98) | copy-start | bytes 772
  60.0 18.4 %copy-start.20 = (pred[256]{0:T(512)(128)(4,1)S(1)}, pred[256]{0:T(512)(128)(4,1)}, u32[]{:S(2)}) copy-start(pred[256]{0:T(512)(128)(4,1)} %get-tuple-element.99) | copy-start | bytes 772
  98.9 1.5 %copy-start.6 = (f32[2,2,24,10,80]{4,2,3,1,0:T(8,128)S(1)}, f32[2,2,24,10,80]{4,2,3,1,0:T(8,128)}, u32[]{:S(2)}) copy-start(f32[2,2,24,10,80]{4,2,3,1,0:T(8,128)} %copy-done.5) | copy-start | bytes 921604
  98.9 1.5 %copy-start.8 = (f32[2,2,24,10,80]{4,2,3,1,0:T(8,128)S(1)}, f32[2,2,24,10,80]{4,2,3,1,0:T(8,128)}, u32[]{:S(2)}) copy-start(f32[2,2,24,10,80]{4,2,3,1,0:T(8,128)} %copy-done.7) | copy-start | bytes 921604
  136.6 3.2 %copy-start.23 = (s32[4]{0:T(128)S(1)}, s32[4]{0:T(128)}, u32[]{:S(2)}) copy-start(s32[4]{0:T(128)} %broadcast_maximum_fusion) | copy-start | bytes 52
  138.0 6.5 %collective-permute-start.9 = (f32[2,24,8,64]{3,2,1,0:T(8,128)S(1)}, f32[2,24,8,64]{3,2,1,0:T(8,128)S(1)}, u32[]{:S(2)}, u32[]{:S(2)}) collective-permute-start(f32[2,24,8,64]{3,2,1,0:T(8,128)S(1)} %get-tuple-element.65), channel_id=1, source_target_pairs={{0,30},{2,0},{4,2},{6,4},{8,6},{10,8},{12,10},{14,12},{16,14},{18,... | collective-permute-start | bytes 294920 | tf_op jit(solution)/shard_map/ppermute | solution.py:29
  141.4 3.7 %copy-start.24 = (pred[4]{0:T(512)(128)(4,1)S(1)}, pred[4]{0:T(512)(128)(4,1)}, u32[]{:S(2)}) copy-start(pred[4]{0:T(512)(128)(4,1)} %get-tuple-element.91) | copy-start | bytes 16
  141.4 3.8 %copy-start.4 = (f32[24,16,128]{2,0,1:T(8,128)S(1)}, f32[24,16,128]{2,0,1:T(8,128)}, u32[]{:S(2)}) copy-start(f32[24,16,128]{2,0,1:T(8,128)} %copy-done.3) | copy-start | bytes 589828
  (5 other events, 5.0 us)
where the time goes:
time: 149 us
  local copies, waits for them, and re-layouts  63.8 us (43%)
  other arithmetic  28.2 us (19%)
  waiting for transfers between devices  22.2 us (15%)
  matrix products  17.7 us (12%)
  starting transfers between devices  15.8 us (11%)
    scatter x2, local copies, waits for them, and re-layouts, pad_from_cycle(): return cut.at[..., 1:-1, fine_depth:-fine_depth].set(patches)  36.5 us
    ppermute x2, waiting for transfers between devices, shifted(): return lax.ppermute(value, axis, pairs)  18.8 us
    sub x2, other arithmetic, transport(): return center + diffusion * laplacian - courant * (center - lower_z)  16.4 us
    dot_general x12, matrix products, react(): jnp.einsum('fg,...gxm->...fxm', reaction, fields, precision=highest_mode)  15.1 us
    ppermute x4, starting transfers between devices, padded_2(): after = lax.ppermute(leading, axis, down)  10.7 us
    slice x6, local copies, waits for them, and re-layouts, roll_depth(): jnp.roll(center, 1, axis=-1)  7.47 us
    slice x6, local copies, waits for them, and re-layouts, roll_depth(): jnp.roll(center, 1 - depth, axis=-1)  7 us
    unnamed x60, local copies, waits for them, and re-layouts  5.59 us
  transfers between devices with their start and end apart: 10, of which 7 were waited for; matrix products, arithmetic and copies ran while one was open for 12% of the time, Pallas kernels for 0%

commit v1 on v0

v1 whole, which is shorter than its diff:
```python
import functools
import jax
import jax.numpy as jnp
from jax import lax
from jax.experimental import pallas as pl
from jax.experimental.pallas import tpu as pltpu
from jax.sharding import PartitionSpec as P

MESH = pl.DeviceIdType.MESH
F32 = jnp.float32
BF16 = jnp.bfloat16


def lanes(rows):
    return lax.broadcasted_iota(jnp.int32, (rows, 128), 1)


def pick(table, index):
    return jnp.take_along_axis(table, index, axis=1)


def powers(reaction, fields):
    row = lax.broadcasted_iota(jnp.int32, (fields, 3 * fields), 0)
    col = lax.broadcasted_iota(jnp.int32, (fields, 3 * fields), 1)
    power = (col % fields == row).astype(F32)
    result = []
    for _ in range(4):
        power = jnp.dot(
            reaction, power, precision=lax.Precision.HIGHEST, preferred_element_type=F32
        )
        result.append(power)
    return result, col < 2 * fields


def chem_weights(power_list, high_part, step):
    parts = []
    for count, (choose, power) in enumerate(zip((4.0, 6.0, 4.0, 1.0), power_list)):
        value = power * (choose * step ** (count + 1))
        high = value.astype(BF16).astype(F32)
        parts.append(jnp.where(high_part, high, value - high))
    return jnp.concatenate(parts, axis=0).astype(BF16)


def chemistry(weights, values, rates, fields):
    wide = jnp.concatenate(values, axis=1)
    high = wide.astype(BF16).astype(F32)
    low = wide - high
    stacked = jnp.concatenate([high, low, high], axis=0).astype(BF16)
    product = jnp.dot(weights, stacked, preferred_element_type=F32)
    out = []
    for n, (value, rate) in enumerate(zip(values, rates)):
        part = [
            product[q * fields : (q + 1) * fields, n * 128 : (n + 1) * 128] for q in range(4)
        ]
        rate = jnp.broadcast_to(rate, value.shape)
        out.append(value + rate * (part[0] + rate * (part[1] + rate * (part[2] + rate * part[3]))))
    return out


def kernel(
    n_gx, n_gy, fields, size_x, slots,
    refine_ref, parent_ref, coarse_hbm, crate_hbm, fine_hbm, frate_hbm, kappa_ref, reaction_ref,
    coarse_out_hbm, fine_out_hbm,
    cin, crate, fin, frate, fout, cout,
    buf_a, buf_b, row_send, col_send, hx, hy, cnew, cols, ring_local, ring_send, ring_recv,
    means, mean_send, mean_recv, wf_ref, wc_ref, rate8,
    in_sem, out_sem, send_sem, recv_sem,
):
    F = fields
    gx = lax.axis_index("gx")
    gy = lax.axis_index("gy")
    right = lax.rem(gx + 1, n_gx)
    left = lax.rem(gx + n_gx - 1, n_gx)
    above = lax.rem(gy + 1, n_gy)
    below = lax.rem(gy + n_gy - 1, n_gy)

    loads = [
        pltpu.make_async_copy(coarse_hbm, cin, in_sem.at[0]),
        pltpu.make_async_copy(crate_hbm, crate, in_sem.at[1]),
        pltpu.make_async_copy(frate_hbm, frate, in_sem.at[2]),
    ]
    fine_loads = []
    for s in range(slots):
        for h in range(2):
            fine_loads.append(
                pltpu.make_async_copy(
                    fine_hbm.at[s, :, pl.ds(h * 128, 128)], fin.at[s, h], in_sem.at[3 + 2 * s + h]
                )
            )
    for copy in loads + fine_loads:
        copy.start()

    barrier = pltpu.get_barrier_semaphore()
    for target in ((left, gy), (right, gy), (gx, below), (gx, above)):
        pl.semaphore_signal(barrier, inc=1, device_id=target, device_id_type=MESH)

    def send(n, src, dst, target):
        copy = pltpu.make_async_remote_copy(
            src_ref=src, dst_ref=dst, send_sem=send_sem.at[n], recv_sem=recv_sem.at[n],
            device_id=target, device_id_type=MESH,
        )
        copy.start()
        return copy

    lane = lanes(F)
    first_half = lane < 64

    def pack(rows_of, y):
        total = jnp.zeros((F, 128), F32)
        for x in range(size_x):
            shift = ((x - y) * 8) % 128
            row = rows_of(x)
            moved = pltpu.roll(row, shift, 1) if shift else row
            total = jnp.where(lane // 8 == x, moved, total)
        return total

    def halos(level):
        base = 4 * level
        return [
            send(base + 0, row_send.at[level, 1], hx.at[level, 0], (right, gy)),
            send(base + 1, row_send.at[level, 0], hx.at[level, 1], (left, gy)),
            send(base + 2, col_send.at[level, 1], hy.at[level, 0], (gx, above)),
            send(base + 3, col_send.at[level, 0], hy.at[level, 1], (gx, below)),
        ]

    loads[0].wait()
    old_rows = lambda x: cin[pl.ds(x, F, stride=size_x), :]
    row_send[0, 0] = old_rows(0)
    row_send[0, 1] = old_rows(size_x - 1)
    col_send[0, 0] = pack(old_rows, 0)
    col_send[0, 1] = pack(old_rows, size_x - 1)
    pl.semaphore_wait(barrier, 4)
    pending = halos(0)
    old_halos = pending

    cols[0, 0] = pack(old_rows, size_x // 2 - 1)
    cols[0, 1] = pack(old_rows, size_x // 2)
    power_list, high_part = powers(reaction_ref[...], F)
    wf_ref[...] = chem_weights(power_list, high_part, 0.125)
    wc_ref[...] = chem_weights(power_list, high_part, 0.25)
    diag = lax.broadcasted_iota(jnp.int32, (F, F), 0) == lax.broadcasted_iota(jnp.int32, (F, F), 1)
    kappa_col = jnp.sum(
        jnp.where(diag, jnp.broadcast_to(kappa_ref[...], (F, F)), 0.0), axis=1, keepdims=True
    )
    kappa = jnp.broadcast_to(kappa_col, (F, 128))
    kappa2 = 2.0 * kappa

    for copy in fine_loads:
        copy.wait()
    for s in range(slots):
        for h in range(2):
            for x in range(size_x):
                buf_a[s, x + 1, :, pl.ds(h * 128, 128)] = fin[s, h, pl.ds(x, F, stride=size_x), :]
    loads[1].wait()
    loads[2].wait()
    for s in range(slots):
        for x in range(size_x):
            rate8[s, x] = jnp.broadcast_to(frate[s, pl.ds(x, 1), :], rate8.shape[2:])

    for copy in old_halos:
        copy.wait_recv()

    z8 = lane % 8
    for group in range(size_x // 4):
        values, rates = [], []
        for x in range(4 * group, 4 * group + 4):
            c = old_rows(x)
            up = old_rows(x - 1) if x > 0 else hx[0, 0]
            dn = old_rows(x + 1) if x < size_x - 1 else hx[0, 1]
            ghost_lo = pltpu.roll(hy[0, 0], (-x * 8) % 128, 1) if x else hy[0, 0]
            shift = (120 - x * 8) % 128
            ghost_hi = pltpu.roll(hy[0, 1], shift, 1) if shift else hy[0, 1]
            yl = jnp.where(lane < 8, ghost_lo, pltpu.roll(c, 8, 1))
            yh = jnp.where(lane >= 120, ghost_hi, pltpu.roll(c, 120, 1))
            zl = jnp.where(z8 == 0, pltpu.roll(c, 121, 1), pltpu.roll(c, 1, 1))
            zu = jnp.where(z8 == 7, pltpu.roll(c, 7, 1), pltpu.roll(c, 127, 1))
            lap = (yl + yh) + (up + dn) + (zl + zu) - 6.0 * c
            values.append(c + kappa * lap - 0.25 * (c - zl))
            rates.append(crate[pl.ds(x, 1), :])
        for n, new in enumerate(chemistry(wc_ref[...], values, rates, F)):
            cnew[4 * group + n] = new
    new_rows = lambda x: cnew[x]
    row_send[1, 0] = new_rows(0)
    row_send[1, 1] = new_rows(size_x - 1)
    col_send[1, 0] = pack(new_rows, 0)
    col_send[1, 1] = pack(new_rows, size_x - 1)
    new_halos = halos(1)

    parents = [jnp.full((F, 128), refine_ref[p], jnp.int32) for p in range(4)]

    def rings(level, rows_of):
        mid = size_x // 2
        row_at = (hx[level, 0], rows_of(mid - 1), rows_of(mid), hx[level, 1])
        col_at = (hy[level, 0], cols[level, 0], cols[level, 1], hy[level, 1])

        def joined(lo, hi, half):
            if half == 0:
                return jnp.where(first_half, lo, pltpu.roll(hi, 64, 1))
            return jnp.where(first_half, pltpu.roll(lo, 64, 1), hi)

        all_rings = []
        for p in range(4):
            a, b = p // 2, p % 2
            all_rings.append(
                (joined(row_at[a], row_at[a + 2], b), joined(col_at[b], col_at[b + 2], a))
            )
        for k in range(4):
            for side in range(2):
                value = jnp.zeros((F, 128), F32)
                for p in range(4):
                    value = jnp.where(parents[p] == k, all_rings[p][side], value)
                if k < 2:
                    ring_local[level, k, side] = value
                else:
                    ring_send[level, k - 2, side] = value
        return send(8 + level, ring_send.at[level], ring_recv.at[level], (right, gy))

    ring_old = rings(0, old_rows)
    cols[1, 0] = pack(new_rows, size_x // 2 - 1)
    cols[1, 1] = pack(new_rows, size_x // 2)

    z16 = lane % 16
    row_index = (lane // 32) * 8 + z16 // 2
    col_index = jnp.where(lane < 64, 0, 64) + z16 // 2
    target = lane % 64
    mean_index = ((target // 8) % 4) * 32 + 2 * (target % 8)
    mean_low = target // 32 == 0

    def ring_of(level, s, side):
        return ring_local[level, s, side] if s < 2 else ring_recv[level, s - 2, side]

    def fine_step(s, step):
        src = buf_a if step == 0 else buf_b
        if step == 0:
            edge_x, edge_y = ring_of(0, s, 0), ring_of(0, s, 1)
        else:
            edge_x = 0.5 * (ring_of(0, s, 0) + ring_of(1, s, 0))
            edge_y = 0.5 * (ring_of(0, s, 1) + ring_of(1, s, 1))
        for h in range(2):
            src[s, 0, :, pl.ds(h * 128, 128)] = pick(edge_x, row_index + 32 * h)
            src[s, size_x + 1, :, pl.ds(h * 128, 128)] = pick(edge_x, row_index + 64 + 32 * h)
        weights = wf_ref[...]
        live = jnp.full((F, 128), parent_ref[s], jnp.int32) >= 0

        def pair(j, carry):
            ghost = pick(edge_y, col_index + 8 * j)
            values, rates = [], []
            for n in range(2):
                x = 2 * j + n
                c = [src[s, x + 1, :, pl.ds(h * 128, 128)] for h in range(2)]
                up = [src[s, x, :, pl.ds(h * 128, 128)] for h in range(2)]
                dn = [src[s, x + 2, :, pl.ds(h * 128, 128)] for h in range(2)]
                ra = [pltpu.roll(v, 16, 1) for v in c]
                rb = [pltpu.roll(v, 112, 1) for v in c]
                yl = [jnp.where(lane < 16, ghost, ra[0]), jnp.where(lane < 16, ra[0], ra[1])]
                yh = [jnp.where(lane >= 112, rb[1], rb[0]), jnp.where(lane >= 112, ghost, rb[1])]
                for h in range(2):
                    v = c[h]
                    zl = jnp.where(z16 == 0, pltpu.roll(v, 113, 1), pltpu.roll(v, 1, 1))
                    zu = jnp.where(z16 == 15, pltpu.roll(v, 15, 1), pltpu.roll(v, 127, 1))
                    lap = (yl[h] + yh[h]) + (up[h] + dn[h]) + (zl + zu) - 6.0 * v
                    values.append(v + kappa2 * lap - 0.25 * (v - zl))
                    rate = rate8[s, x, :, pl.ds(h * 128, 128)]
                    rates.append(jnp.concatenate([rate] * (F // 8), axis=0))
            new = chemistry(weights, values, rates, F)
            if step == 0:
                for n in range(2):
                    for h in range(2):
                        buf_b[s, 2 * j + n + 1, :, pl.ds(h * 128, 128)] = new[2 * n + h]
            else:
                new = [jnp.where(live, v, 0.0) for v in new]
                for n in range(2):
                    for h in range(2):
                        fout[s, h, pl.ds(2 * j + n, F, stride=size_x), :] = new[2 * n + h]
                picked = []
                for h in range(2):
                    total = new[h] + new[2 + h]
                    total = total + pltpu.roll(total, 127, 1)
                    total = total + pltpu.roll(total, 112, 1)
                    picked.append(pick(total, mean_index))
                means[s, j] = 0.125 * jnp.where(mean_low, picked[0], picked[1])
            return carry

        lax.fori_loop(0, size_x // 2, pair, 0)

    stores = []

    def store(s):
        for h in range(2):
            copy = pltpu.make_async_copy(
                fout.at[s, h], fine_out_hbm.at[s, :, pl.ds(h * 128, 128)], out_sem.at[2 * s + h]
            )
            copy.start()
            stores.append(copy)

    half = size_x // 4

    def send_means(s):
        for j in range(half):
            mean_send[s - 2, j] = jnp.where(first_half, means[s, j], means[s, j + half])
        return send(8 + s, mean_send.at[s - 2], mean_recv.at[s - 2], (left, gy))

    fine_step(0, 0)
    fine_step(1, 0)
    for copy in new_halos:
        copy.wait_recv()
    ring_new = rings(1, new_rows)
    fine_step(0, 1)
    store(0)
    ring_old.wait_recv()
    fine_step(2, 0)
    fine_step(3, 0)
    ring_new.wait_recv()
    fine_step(2, 1)
    sent_2 = send_means(2)
    store(2)
    fine_step(3, 1)
    sent_3 = send_means(3)
    store(3)
    fine_step(1, 1)
    store(1)
    sent_2.wait_recv()
    sent_3.wait_recv()

    for x in range(size_x):
        a, X = x // (size_x // 2), x % (size_x // 2)
        full = [means[0, X], means[1, X]]
        for k in range(2):
            packed = mean_recv[k, X % half]
            turned = pltpu.roll(packed, 64, 1)
            low, high = (packed, turned) if X < half else (turned, packed)
            full.append(jnp.where(first_half, low, high))
        owner = jnp.where(first_half, parents[2 * a], parents[2 * a + 1])
        value = new_rows(x)
        for k in range(4):
            value = jnp.where(owner == k, full[k], value)
        cout[pl.ds(x, F, stride=size_x), :] = value
    last = pltpu.make_async_copy(cout, coarse_out_hbm, out_sem.at[8])
    last.start()
    stores.append(last)
    for copy in old_halos + new_halos + [ring_old, ring_new, sent_2, sent_3]:
        copy.wait_send()
    for copy in stores:
        copy.wait()


def body(coarse_state, coarse_rate, fine_state, fine_rate, refine_to, parent_of, kappa, reaction):
    fields, size_x, merged = coarse_state.shape
    slots = fine_state.shape[0]
    fine_merged = fine_state.shape[3]
    flat = fields * size_x
    any_spec = pl.BlockSpec(memory_space=pl.ANY)
    smem = pl.BlockSpec(memory_space=pltpu.SMEM)
    vmem = pl.BlockSpec(memory_space=pltpu.VMEM)
    V = pltpu.VMEM
    tile = (fields, 128)
    coarse_out, fine_out = pl.pallas_call(
        functools.partial(
            kernel, lax.axis_size("gx"), lax.axis_size("gy"), fields, size_x, slots
        ),
        out_shape=(
            jax.ShapeDtypeStruct((flat, merged), F32),
            jax.ShapeDtypeStruct((slots, flat, fine_merged), F32),
        ),
        in_specs=[smem, smem, any_spec, any_spec, any_spec, any_spec, vmem, vmem],
        out_specs=(any_spec, any_spec),
        scratch_shapes=[
            V((flat, 128), F32),
            V((size_x, 128), F32),
            V((slots, 2, flat, 128), F32),
            V((slots, size_x, fine_merged), F32),
            V((slots, 2, flat, 128), F32),
            V((flat, 128), F32),
            V((slots, size_x + 2, fields, fine_merged), F32),
            V((slots, size_x + 2, fields, fine_merged), F32),
            V((2, 2) + tile, F32),
            V((2, 2) + tile, F32),
            V((2, 2) + tile, F32),
            V((2, 2) + tile, F32),
            V((size_x,) + tile, F32),
            V((2, 2) + tile, F32),
            V((2, 2, 2) + tile, F32),
            V((2, 2, 2) + tile, F32),
            V((2, 2, 2) + tile, F32),
            V((slots, size_x // 2) + tile, F32),
            V((2, size_x // 4) + tile, F32),
            V((2, size_x // 4) + tile, F32),
            V((4 * fields, 3 * fields), BF16),
            V((4 * fields, 3 * fields), BF16),
            V((slots, size_x, 8, fine_merged), F32),
            pltpu.SemaphoreType.DMA((11,)),
            pltpu.SemaphoreType.DMA((9,)),
            pltpu.SemaphoreType.DMA((12,)),
            pltpu.SemaphoreType.DMA((12,)),
        ],
        compiler_params=pltpu.CompilerParams(
            collective_id=0, has_side_effects=True, vmem_limit_bytes=48 * 1024 * 1024
        ),
    )(
        refine_to, parent_of, coarse_state.reshape(flat, merged), coarse_rate,
        fine_state.reshape(slots, flat, fine_merged), fine_rate, kappa.reshape(1, fields), reaction,
    )
    return coarse_out.reshape(coarse_state.shape), fine_out.reshape(fine_state.shape)


def solution(mesh):
    in_specs = (
        P(None, "gx", "gy"),
        P("gx", "gy"),
        P(("gx", "gy"), None, None, None),
        P(("gx", "gy"), None, None),
        P(("gx", "gy")),
        P(("gx", "gy")),
        P(),
        P(),
    )
    out_specs = (P(None, "gx", "gy"), P(("gx", "gy"), None, None, None))
    return jax.shard_map(body, mesh=mesh, in_specs=in_specs, out_specs=out_specs, check_vma=False)
```

time: 149 us -> 51.3 us (0.34)
  local copies, waits for them, and re-layouts: 63.8 us -> 8.35 us
  Pallas kernels: 0 us -> 41.9 us
  other arithmetic: 28.2 us -> 0 us
  waiting for transfers between devices: 22.2 us -> 0 us
  matrix products: 17.7 us -> 0 us
  starting transfers between devices: 15.8 us -> 0 us
    pallas_call x0 -> x1, Pallas kernels: none -> 41.9 us  [body(): pl.pallas_call(functools.partial(kernel, lax.axis_size('gx'), lax.axis_si...]
    scatter x2 -> x0, local copies, waits for them, and re-layouts: 36.5 us -> none  [pad_from_cycle(): return cut.at[..., 1:-1, fine_depth:-fine_depth].set(patches)]
    ppermute x10 -> x0, waiting for transfers between devices: 22.2 us -> none  [the longest x2 18.8 us: shifted(): return lax.ppermute(value, axis, pairs)]
    slice x21 -> x0, local copies, waits for them, and re-layouts: 19.9 us -> none  [the longest x6 7.47 us: roll_depth(): jnp.roll(center, 1, axis=-1)]
    dot_general x15 -> x0, matrix products: 17.7 us -> none  [the longest x12 15.1 us: react(): jnp.einsum('fg,...gxm->...fxm', reaction, fields, precision=highest_mode)]
    sub x2 -> x0, other arithmetic: 16.4 us -> none  [transport(): return center + diffusion * laplacian - courant * (center - lower_z)]
    ppermute x10 -> x0, starting transfers between devices: 15.8 us -> none  [the longest x4 10.7 us: padded_2(): after = lax.ppermute(leading, axis, down)]
    select_n x8 -> x0, other arithmetic: 5.37 us -> none  [the longest x1 2.7 us: body(): col_blocks.append(jnp.where(refined[parent], averaged[parent], own))]
  transfers between devices with their start and end apart: 10 -> 0, of which waited for: 7 -> 0; matrix products, arithmetic and copies ran while one was open for 12% -> 0% of each run, Pallas kernels for 0% -> 0%
where the time goes in v1:
time: 51.3 us; the launch traced here: 50.9 us
  Pallas kernels  41.9 us (82%)
  local copies, waits for them, and re-layouts  8.35 us (16%)
  between operations  0.66 us (1%)
    pallas_call x1, Pallas kernels, body(): pl.pallas_call(functools.partial(kernel, lax.axis_size('gx'), lax.axis_si...  41.9 us
    unnamed x18, local copies, waits for them, and re-layouts  8.35 us

profile of v1, /device:TPU:0, one launch (start us, length us, event | category | flops | bytes accessed | tf_op | source)
XLA Modules:
  0.0 50.9 jit_solution(12475641838923187307)
XLA Ops:
  0.6 0.0 copy-start
  0.6 1.4 %copy-done = f32[4,24,16,256]{3,2,1,0:T(8,128)S(1)} copy-done((f32[4,24,16,256]{3,2,1,0:T(8,128)S(1)}, f32[4,24,16,256]{3,2,1,0:T(8,128)}, u32[]{:S(2)}) %copy-start) | copy-done | bytes 1572888
  2.0 0.0 copy-start.1
  2.0 0.9 %copy-done.1 = f32[24,16,128]{2,1,0:T(8,128)S(1)} copy-done((f32[24,16,128]{2,1,0:T(8,128)S(1)}, f32[24,16,128]{2,1,0:T(8,128)}, u32[]{:S(2)}) %copy-start.1) | copy-done | bytes 196632
  3.0 0.0 copy-start.2
  3.0 0.8 %copy-done.2 = f32[4,16,256]{2,1,0:T(8,128)S(1)} copy-done((f32[4,16,256]{2,1,0:T(8,128)S(1)}, f32[4,16,256]{2,1,0:T(8,128)}, u32[]{:S(2)}) %copy-start.2) | copy-done | bytes 65560
  3.8 0.0 copy-start.3
  3.8 0.7 %copy-done.3 = f32[24,24]{1,0:T(8,128)S(1)} copy-done((f32[24,24]{1,0:T(8,128)S(1)}, f32[24,24]{1,0:T(8,128)}, u32[]{:S(2)}) %copy-start.3) | copy-done | bytes 2328
  4.5 0.0 copy-start.4
  4.5 0.7 %copy-done.4 = f32[16,128]{1,0:T(8,128)S(1)} copy-done((f32[16,128]{1,0:T(8,128)S(1)}, f32[16,128]{1,0:T(8,128)}, u32[]{:S(2)}) %copy-start.4) | copy-done | bytes 8216
  5.2 0.0 copy-start.5
  5.2 0.7 %copy-done.5 = s32[4]{0:T(128)S(1)} copy-done((s32[4]{0:T(128)S(1)}, s32[4]{0:T(128)}, u32[]{:S(2)}) %copy-start.5) | copy-done | bytes 40
  5.9 0.0 copy-start.6
  5.9 0.7 %copy-done.6 = s32[4]{0:T(128)S(1)} copy-done((s32[4]{0:T(128)S(1)}, s32[4]{0:T(128)}, u32[]{:S(2)}) %copy-start.6) | copy-done | bytes 40
  6.5 0.0 copy-start.7
  6.5 0.7 %copy-done.7 = f32[24]{0:T(128)S(1)} copy-done((f32[24]{0:T(128)S(1)}, f32[24]{0:T(128)}, u32[]{:S(2)}) %copy-start.7) | copy-done | bytes 120
  7.2 41.9 %shard_map.95 = (f32[384,128]{1,0:T(8,128)S(1)}, f32[4,384,256]{2,1,0:T(8,128)S(1)}) custom-call(s32[4]{0:T(128)S(1)} %copy-done.5, s32[4]{0:T(128)S(1)} %copy-done.6, f32[384,128]{1,0:T(8,128)S(1)} %bitcast.8, f32[16,128]{1,0:T(8,128)S(1)} %copy-done.4, f32[4,384,256]{2,1,0:T(8,128)S(1)} %bitcast.6, f32[4,16,256]{2,1,0:T(8,128)S(1)} %copy-done.2, ...), custom_call_target="tpu_custom_call" | custom-call | tf_op jit(solution)/shard_map/pallas_call | solution.py:357
  49.1 0.7 %copy.12 = f32[24,16,128]{2,1,0:T(8,128)} copy(f32[24,16,128]{2,1,0:T(8,128)S(1)} %bitcast.7) | data formatting | bytes 393216
  49.8 1.1 %copy.13 = f32[4,24,16,256]{3,2,1,0:T(8,128)} copy(f32[4,24,16,256]{3,2,1,0:T(8,128)S(1)} %bitcast.5) | data formatting | bytes 3145728
Async XLA Ops:
  0.6 1.4 %copy-start = (f32[4,24,16,256]{3,2,1,0:T(8,128)S(1)}, f32[4,24,16,256]{3,2,1,0:T(8,128)}, u32[]{:S(2)}) copy-start(f32[4,24,16,256]{3,2,1,0:T(8,128)} %param.10) | copy-start | bytes 4718596
  2.0 0.9 %copy-start.1 = (f32[24,16,128]{2,1,0:T(8,128)S(1)}, f32[24,16,128]{2,1,0:T(8,128)}, u32[]{:S(2)}) copy-start(f32[24,16,128]{2,1,0:T(8,128)} %param.8) | copy-start | bytes 589828
  3.0 0.8 %copy-start.2 = (f32[4,16,256]{2,1,0:T(8,128)S(1)}, f32[4,16,256]{2,1,0:T(8,128)}, u32[]{:S(2)}) copy-start(f32[4,16,256]{2,1,0:T(8,128)} %frate_hbm.1) | copy-start | bytes 196612
  3.8 0.7 %copy-start.3 = (f32[24,24]{1,0:T(8,128)S(1)}, f32[24,24]{1,0:T(8,128)}, u32[]{:S(2)}) copy-start(f32[24,24]{1,0:T(8,128)} %reaction_ref.1) | copy-start | bytes 6916
  4.5 0.7 %copy-start.4 = (f32[16,128]{1,0:T(8,128)S(1)}, f32[16,128]{1,0:T(8,128)}, u32[]{:S(2)}) copy-start(f32[16,128]{1,0:T(8,128)} %crate_hbm.1) | copy-start | bytes 24580
  5.2 0.7 %copy-start.5 = (s32[4]{0:T(128)S(1)}, s32[4]{0:T(128)}, u32[]{:S(2)}) copy-start(s32[4]{0:T(128)} %refine_ref.1) | copy-start | bytes 52
  5.9 0.7 %copy-start.6 = (s32[4]{0:T(128)S(1)}, s32[4]{0:T(128)}, u32[]{:S(2)}) copy-start(s32[4]{0:T(128)} %parent_ref.1) | copy-start | bytes 52
  6.5 0.7 %copy-start.7 = (f32[24]{0:T(128)S(1)}, f32[24]{0:T(128)}, u32[]{:S(2)}) copy-start(f32[24]{0:T(128)} %param.14) | copy-start | bytes 292

commit v2 on v1

--- a/solution.py
+++ b/solution.py
@@ -394,7 +394,7 @@
             pltpu.SemaphoreType.DMA((12,)),
         ],
         compiler_params=pltpu.CompilerParams(
-            collective_id=0, has_side_effects=True, vmem_limit_bytes=48 * 1024 * 1024
+            collective_id=0, has_side_effects=True, vmem_limit_bytes=67043328
         ),
     )(
         refine_to, parent_of, coarse_state.reshape(flat, merged), coarse_rate,

time: 51.3 us -> 47.1 us (0.918)
  local copies, waits for them, and re-layouts: 8.35 us -> 4.28 us
    unnamed x18 -> x2, local copies, waits for them, and re-layouts: 8.35 us -> 4.28 us
where the time goes in v2:
time: 47.1 us; the launch traced here: 46.9 us
  Pallas kernels  41.9 us (89%)
  local copies, waits for them, and re-layouts  4.28 us (9%)
  between operations  0.64 us (1%)
    pallas_call x1, Pallas kernels, body(): pl.pallas_call(functools.partial(kernel, lax.axis_size('gx'), lax.axis_si...  41.9 us
    unnamed x2, local copies, waits for them, and re-layouts  4.28 us

profile of v2, /device:TPU:0, one launch (start us, length us, event | category | flops | bytes accessed | tf_op | source)
XLA Modules:
  0.0 46.9 jit_solution(13539267757246201738)
XLA Ops:
  0.6 41.9 %shard_map.95 = (f32[384,128]{1,0:T(8,128)}, f32[4,384,256]{2,1,0:T(8,128)}) custom-call(s32[4]{0:T(128)} %refine_ref.1, s32[4]{0:T(128)} %parent_ref.1, f32[384,128]{1,0:T(8,128)} %bitcast.8, f32[16,128]{1,0:T(8,128)} %crate_hbm.1, f32[4,384,256]{2,1,0:T(8,128)} %bitcast.6, f32[4,16,256]{2,1,0:T(8,128)} %frate_hbm.1, f32[1,24]{1,0:T(1,128)} %bitcast.9, ...), custom_call_target="tpu_custom_call" | custom-call | tf_op jit(solution)/shard_map/pallas_call | solution.py:357
  42.6 1.6 %copy.12 = f32[24,16,128]{2,1,0:T(8,128)} copy(f32[24,16,128]{2,1,0:T(8,128)} %bitcast.7) | data formatting | bytes 393216
  44.2 2.7 %copy.13 = f32[4,24,16,256]{3,2,1,0:T(8,128)} copy(f32[4,24,16,256]{3,2,1,0:T(8,128)} %bitcast.5) | data formatting | bytes 3145728

commit v3 on v2

--- a/solution.py
+++ b/solution.py
@@ -63,10 +63,11 @@
     coarse_out_hbm, fine_out_hbm,
     cin, crate, fin, frate, fout, cout,
     buf_a, buf_b, row_send, col_send, hx, hy, cnew, cols, ring_local, ring_send, ring_recv,
-    means, mean_send, mean_recv, wf_ref, wc_ref, rate8,
+    means, mean_send, mean_recv, wf_ref, wc_ref, rate8, edge_rate,
     in_sem, out_sem, send_sem, recv_sem,
 ):
     F = fields
+    fine_cols = frate.shape[2]
     gx = lax.axis_index("gx")
     gy = lax.axis_index("gy")
     right = lax.rem(gx + 1, n_gx)
@@ -129,9 +130,6 @@
     row_send[0, 1] = old_rows(size_x - 1)
     col_send[0, 0] = pack(old_rows, 0)
     col_send[0, 1] = pack(old_rows, size_x - 1)
-    pl.semaphore_wait(barrier, 4)
-    pending = halos(0)
-    old_halos = pending
 
     cols[0, 0] = pack(old_rows, size_x // 2 - 1)
     cols[0, 1] = pack(old_rows, size_x // 2)
@@ -156,69 +154,19 @@
     for s in range(slots):
         for x in range(size_x):
             rate8[s, x] = jnp.broadcast_to(frate[s, pl.ds(x, 1), :], rate8.shape[2:])
-
-    for copy in old_halos:
-        copy.wait_recv()
-
-    z8 = lane % 8
-    for group in range(size_x // 4):
-        values, rates = [], []
-        for x in range(4 * group, 4 * group + 4):
-            c = old_rows(x)
-            up = old_rows(x - 1) if x > 0 else hx[0, 0]
-            dn = old_rows(x + 1) if x < size_x - 1 else hx[0, 1]
-            ghost_lo = pltpu.roll(hy[0, 0], (-x * 8) % 128, 1) if x else hy[0, 0]
-            shift = (120 - x * 8) % 128
-            ghost_hi = pltpu.roll(hy[0, 1], shift, 1) if shift else hy[0, 1]
-            yl = jnp.where(lane < 8, ghost_lo, pltpu.roll(c, 8, 1))
-            yh = jnp.where(lane >= 120, ghost_hi, pltpu.roll(c, 120, 1))
-            zl = jnp.where(z8 == 0, pltpu.roll(c, 121, 1), pltpu.roll(c, 1, 1))
-            zu = jnp.where(z8 == 7, pltpu.roll(c, 7, 1), pltpu.roll(c, 127, 1))
-            lap = (yl + yh) + (up + dn) + (zl + zu) - 6.0 * c
-            values.append(c + kappa * lap - 0.25 * (c - zl))
-            rates.append(crate[pl.ds(x, 1), :])
-        for n, new in enumerate(chemistry(wc_ref[...], values, rates, F)):
-            cnew[4 * group + n] = new
-    new_rows = lambda x: cnew[x]
-    row_send[1, 0] = new_rows(0)
-    row_send[1, 1] = new_rows(size_x - 1)
-    col_send[1, 0] = pack(new_rows, 0)
-    col_send[1, 1] = pack(new_rows, size_x - 1)
-    new_halos = halos(1)
-
-    parents = [jnp.full((F, 128), refine_ref[p], jnp.int32) for p in range(4)]
-
-    def rings(level, rows_of):
-        mid = size_x // 2
-        row_at = (hx[level, 0], rows_of(mid - 1), rows_of(mid), hx[level, 1])
-        col_at = (hy[level, 0], cols[level, 0], cols[level, 1], hy[level, 1])
-
-        def joined(lo, hi, half):
-            if half == 0:
-                return jnp.where(first_half, lo, pltpu.roll(hi, 64, 1))
-            return jnp.where(first_half, pltpu.roll(lo, 64, 1), hi)
-
-        all_rings = []
-        for p in range(4):
-            a, b = p // 2, p % 2
-            all_rings.append(
-                (joined(row_at[a], row_at[a + 2], b), joined(col_at[b], col_at[b + 2], a))
-            )
-        for k in range(4):
-            for side in range(2):
-                value = jnp.zeros((F, 128), F32)
-                for p in range(4):
-                    value = jnp.where(parents[p] == k, all_rings[p][side], value)
-                if k < 2:
-                    ring_local[level, k, side] = value
-                else:
-                    ring_send[level, k - 2, side] = value
-        return send(8 + level, ring_send.at[level], ring_recv.at[level], (right, gy))
-
-    ring_old = rings(0, old_rows)
-    cols[1, 0] = pack(new_rows, size_x // 2 - 1)
-    cols[1, 1] = pack(new_rows, size_x // 2)
-
+    lane8 = lanes(8)
+    for s in range(slots):
+        for q in range(size_x // 4):
+            total = jnp.zeros((8, 128), F32)
+            for n in range(4):
+                lo = rate8[s, 4 * q + n, :, pl.ds(0, 128)]
+                hi = rate8[s, 4 * q + n, :, pl.ds(fine_cols - 128, 128)]
+                lo = pltpu.roll(lo, 16 * n, 1) if n else lo
+                shift = (16 * n - 48) % 128
+                hi = pltpu.roll(hi, shift, 1) if shift else hi
+                total = jnp.where(lane8 // 16 == n, lo, total)
+                total = jnp.where(lane8 // 16 == 4 + n, hi, total)
+            edge_rate[s, q] = total
     z16 = lane % 16
     row_index = (lane // 32) * 8 + z16 // 2
     col_index = jnp.where(lane < 64, 0, 64) + z16 // 2
@@ -232,18 +180,19 @@
     def fine_step(s, step):
         src = buf_a if step == 0 else buf_b
         if step == 0:
-            edge_x, edge_y = ring_of(0, s, 0), ring_of(0, s, 1)
+            src[s, 0] = jnp.zeros((F, fine_cols), F32)
+            src[s, size_x + 1] = jnp.zeros((F, fine_cols), F32)
         else:
             edge_x = 0.5 * (ring_of(0, s, 0) + ring_of(1, s, 0))
             edge_y = 0.5 * (ring_of(0, s, 1) + ring_of(1, s, 1))
-        for h in range(2):
-            src[s, 0, :, pl.ds(h * 128, 128)] = pick(edge_x, row_index + 32 * h)
-            src[s, size_x + 1, :, pl.ds(h * 128, 128)] = pick(edge_x, row_index + 64 + 32 * h)
+            for h in range(2):
+                src[s, 0, :, pl.ds(h * 128, 128)] = pick(edge_x, row_index + 32 * h)
+                src[s, size_x + 1, :, pl.ds(h * 128, 128)] = pick(edge_x, row_index + 64 + 32 * h)
         weights = wf_ref[...]
         live = jnp.full((F, 128), parent_ref[s], jnp.int32) >= 0
 
         def pair(j, carry):
-            ghost = pick(edge_y, col_index + 8 * j)
+            ghost = pick(edge_y, col_index + 8 * j) if step else jnp.zeros((F, 128), F32)
             values, rates = [], []
             for n in range(2):
                 x = 2 * j + n
@@ -281,7 +230,106 @@
                 means[s, j] = 0.125 * jnp.where(mean_low, picked[0], picked[1])
             return carry
 
-        lax.fori_loop(0, size_x // 2, pair, 0)
+        lax.fori_loop(0, size_x // 2, pair, 0, unroll=4)
+
+    edge_index = (lane // 64) * 64 + ((lane % 64) // 32) * 8 + z16 // 2
+
+    def wide_rate(rate):
+        return jnp.concatenate([rate] * (F // 8), axis=0)
+
+    def correct(s):
+        edge_x, edge_y = ring_of(0, s, 0), ring_of(0, s, 1)
+        values, rates = [], []
+        for side, x in ((0, 0), (1, size_x - 1)):
+            for h in range(2):
+                values.append(kappa2 * pick(edge_x, row_index + 64 * side + 32 * h))
+                rates.append(wide_rate(rate8[s, x, :, pl.ds(h * 128, 128)]))
+        for q in range(size_x // 4):
+            values.append(kappa2 * pick(edge_y, edge_index + 16 * q))
+            rates.append(wide_rate(edge_rate[s, q]))
+        share = chemistry(wf_ref[...], values, rates, F)
+        for x in range(size_x):
+            q, n = x // 4, x % 4
+            both = share[4 + q]
+            lo = pltpu.roll(both, (-16 * n) % 128, 1) if n else both
+            shift = (48 - 16 * n) % 128
+            hi = pltpu.roll(both, shift, 1) if shift else both
+            added = [jnp.where(lane < 16, lo, 0.0), jnp.where(lane >= 112, hi, 0.0)]
+            for h in range(2):
+                if x == 0:
+                    added[h] = added[h] + share[h]
+                if x == size_x - 1:
+                    added[h] = added[h] + share[2 + h]
+                here = (s, x + 1, slice(None), pl.ds(h * 128, 128))
+                buf_b[here] = buf_b[here] + added[h]
+
+    for s in ():
+        fine_step(s, 0)
+    pl.semaphore_wait(barrier, 4)
+    old_halos = halos(0)
+    for s in (0, 1):
+        fine_step(s, 0)
+    for copy in old_halos:
+        copy.wait_recv()
+
+    z8 = lane % 8
+    for group in range(size_x // 4):
+        values, rates = [], []
+        for x in range(4 * group, 4 * group + 4):
+            c = old_rows(x)
+            up = old_rows(x - 1) if x > 0 else hx[0, 0]
+            dn = old_rows(x + 1) if x < size_x - 1 else hx[0, 1]
+            ghost_lo = pltpu.roll(hy[0, 0], (-x * 8) % 128, 1) if x else hy[0, 0]
+            shift = (120 - x * 8) % 128
+            ghost_hi = pltpu.roll(hy[0, 1], shift, 1) if shift else hy[0, 1]
+            yl = jnp.where(lane < 8, ghost_lo, pltpu.roll(c, 8, 1))
+            yh = jnp.where(lane >= 120, ghost_hi, pltpu.roll(c, 120, 1))
+            zl = jnp.where(z8 == 0, pltpu.roll(c, 121, 1), pltpu.roll(c, 1, 1))
+            zu = jnp.where(z8 == 7, pltpu.roll(c, 7, 1), pltpu.roll(c, 127, 1))
+            lap = (yl + yh) + (up + dn) + (zl + zu) - 6.0 * c
+            values.append(c + kappa * lap - 0.25 * (c - zl))
+            rates.append(crate[pl.ds(x, 1), :])
+        for n, new in enumerate(chemistry(wc_ref[...], values, rates, F)):
+            cnew[4 * group + n] = new
+    new_rows = lambda x: cnew[x]
+    row_send[1, 0] = new_rows(0)
+    row_send[1, 1] = new_rows(size_x - 1)
+    col_send[1, 0] = pack(new_rows, 0)
+    col_send[1, 1] = pack(new_rows, size_x - 1)
+    new_halos = halos(1)
+
+    parents = [jnp.full((F, 128), refine_ref[p], jnp.int32) for p in range(4)]
+
+    def rings(level, rows_of):
+        mid = size_x // 2
+        row_at = (hx[level, 0], rows_of(mid - 1), rows_of(mid), hx[level, 1])
+        col_at = (hy[level, 0], cols[level, 0], cols[level, 1], hy[level, 1])
+
+        def joined(lo, hi, half):
+            if half == 0:
+                return jnp.where(first_half, lo, pltpu.roll(hi, 64, 1))
+            return jnp.where(first_half, pltpu.roll(lo, 64, 1), hi)
+
+        all_rings = []
+        for p in range(4):
+            a, b = p // 2, p % 2
+            all_rings.append(
+                (joined(row_at[a], row_at[a + 2], b), joined(col_at[b], col_at[b + 2], a))
+            )
+        for k in range(4):
+            for side in range(2):
+                value = jnp.zeros((F, 128), F32)
+                for p in range(4):
+                    value = jnp.where(parents[p] == k, all_rings[p][side], value)
+                if k < 2:
+                    ring_local[level, k, side] = value
+                else:
+                    ring_send[level, k - 2, side] = value
+        return send(8 + level, ring_send.at[level], ring_recv.at[level], (right, gy))
+
+    ring_old = rings(0, old_rows)
+    cols[1, 0] = pack(new_rows, size_x // 2 - 1)
+    cols[1, 1] = pack(new_rows, size_x // 2)
 
     stores = []
 
@@ -300,16 +348,18 @@
             mean_send[s - 2, j] = jnp.where(first_half, means[s, j], means[s, j + half])
         return send(8 + s, mean_send.at[s - 2], mean_recv.at[s - 2], (left, gy))
 
-    fine_step(0, 0)
-    fine_step(1, 0)
+    for s in (2, 3):
+        fine_step(s, 0)
+    correct(0)
+    correct(1)
     for copy in new_halos:
         copy.wait_recv()
     ring_new = rings(1, new_rows)
     fine_step(0, 1)
     store(0)
     ring_old.wait_recv()
-    fine_step(2, 0)
-    fine_step(3, 0)
+    correct(2)
+    correct(3)
     ring_new.wait_recv()
     fine_step(2, 1)
     sent_2 = send_means(2)
@@ -388,6 +438,7 @@
             V((4 * fields, 3 * fields), BF16),
             V((4 * fields, 3 * fields), BF16),
             V((slots, size_x, 8, fine_merged), F32),
+            V((slots, size_x // 4, 8, 128), F32),
             pltpu.SemaphoreType.DMA((11,)),
             pltpu.SemaphoreType.DMA((9,)),
             pltpu.SemaphoreType.DMA((12,)),

time: 47.1 us -> 33.8 us (0.72)
  Pallas kernels: 41.9 us -> 28.6 us
    pallas_call x1, Pallas kernels: 41.9 us -> 28.6 us  [body(): pl.pallas_call(functools.partial(kernel, lax.axis_size('gx'), lax.axis_si...]
where the time goes in v3:
time: 33.8 us; the launch traced here: 33.5 us
  Pallas kernels  28.6 us (85%)
  local copies, waits for them, and re-layouts  4.28 us (13%)
  between operations  0.64 us (2%)
    pallas_call x1, Pallas kernels, body(): pl.pallas_call(functools.partial(kernel, lax.axis_size('gx'), lax.axis_si...  28.6 us
    unnamed x2, local copies, waits for them, and re-layouts  4.28 us

profile of v3, /device:TPU:0, one launch (start us, length us, event | category | flops | bytes accessed | tf_op | source)
XLA Modules:
  0.0 33.5 jit_solution(2274975733874195334)
XLA Ops:
  0.6 28.6 %shard_map.95 = (f32[384,128]{1,0:T(8,128)}, f32[4,384,256]{2,1,0:T(8,128)}) custom-call(s32[4]{0:T(128)} %refine_ref.1, s32[4]{0:T(128)} %parent_ref.1, f32[384,128]{1,0:T(8,128)} %bitcast.8, f32[16,128]{1,0:T(8,128)} %crate_hbm.1, f32[4,384,256]{2,1,0:T(8,128)} %bitcast.6, f32[4,16,256]{2,1,0:T(8,128)} %frate_hbm.1, f32[1,24]{1,0:T(1,128)} %bitcast.9, ...), custom_call_target="tpu_custom_call" | custom-call | tf_op jit(solution)/shard_map/pallas_call | solution.py:407
  29.3 1.6 %copy.12 = f32[24,16,128]{2,1,0:T(8,128)} copy(f32[24,16,128]{2,1,0:T(8,128)} %bitcast.7) | data formatting | bytes 393216
  30.9 2.7 %copy.13 = f32[4,24,16,256]{3,2,1,0:T(8,128)} copy(f32[4,24,16,256]{3,2,1,0:T(8,128)} %bitcast.5) | data formatting | bytes 3145728

commit v4 on v3

--- a/solution.py
+++ b/solution.py
@@ -191,6 +191,8 @@
         weights = wf_ref[...]
         live = jnp.full((F, 128), parent_ref[s], jnp.int32) >= 0
 
+        own = 0.75 - 6.0 * kappa2
+
         def pair(j, carry):
             ghost = pick(edge_y, col_index + 8 * j) if step else jnp.zeros((F, 128), F32)
             values, rates = [], []
@@ -207,8 +209,8 @@
                     v = c[h]
                     zl = jnp.where(z16 == 0, pltpu.roll(v, 113, 1), pltpu.roll(v, 1, 1))
                     zu = jnp.where(z16 == 15, pltpu.roll(v, 15, 1), pltpu.roll(v, 127, 1))
-                    lap = (yl[h] + yh[h]) + (up[h] + dn[h]) + (zl + zu) - 6.0 * v
-                    values.append(v + kappa2 * lap - 0.25 * (v - zl))
+                    near = (yl[h] + yh[h]) + (up[h] + dn[h]) + (zl + zu)
+                    values.append(own * v + kappa2 * near + 0.25 * zl)
                     rate = rate8[s, x, :, pl.ds(h * 128, 128)]
                     rates.append(jnp.concatenate([rate] * (F // 8), axis=0))
             new = chemistry(weights, values, rates, F)

time: 33.8 us -> 33.8 us (level)
  no operation moved by 1% of the time
where the time goes in v4:
time: 33.8 us; the launch traced here: 33.6 us
  Pallas kernels  28.6 us (85%)
  local copies, waits for them, and re-layouts  4.28 us (13%)
  between operations  0.64 us (2%)
    pallas_call x1, Pallas kernels, body(): pl.pallas_call(functools.partial(kernel, lax.axis_size('gx'), lax.axis_si...  28.6 us
    unnamed x2, local copies, waits for them, and re-layouts  4.28 us

profile of v4, /device:TPU:0, one launch (start us, length us, event | category | flops | bytes accessed | tf_op | source)
XLA Modules:
  0.0 33.6 jit_solution(13689499250183782298)
XLA Ops:
  0.6 28.6 %shard_map.95 = (f32[384,128]{1,0:T(8,128)}, f32[4,384,256]{2,1,0:T(8,128)}) custom-call(s32[4]{0:T(128)} %refine_ref.1, s32[4]{0:T(128)} %parent_ref.1, f32[384,128]{1,0:T(8,128)} %bitcast.8, f32[16,128]{1,0:T(8,128)} %crate_hbm.1, f32[4,384,256]{2,1,0:T(8,128)} %bitcast.6, f32[4,16,256]{2,1,0:T(8,128)} %frate_hbm.1, f32[1,24]{1,0:T(1,128)} %bitcast.9, ...), custom_call_target="tpu_custom_call" | custom-call | tf_op jit(solution)/shard_map/pallas_call | solution.py:409
  29.3 1.6 %copy.12 = f32[24,16,128]{2,1,0:T(8,128)} copy(f32[24,16,128]{2,1,0:T(8,128)} %bitcast.7) | data formatting | bytes 393216
  30.9 2.7 %copy.13 = f32[4,24,16,256]{3,2,1,0:T(8,128)} copy(f32[4,24,16,256]{3,2,1,0:T(8,128)} %bitcast.5) | data formatting | bytes 3145728
